TPU v7x, 256 devices: a whole 4x4x8 slice. The times are simulated.
256 devices in a mesh: gx: 8 (over z), gy: 16 (over y, x), sa: 2 (over core).
Axes of the slice: x: 4, y: 4, z: 8, core: 2. Of those that a mesh axis runs over, the one named last changes fastest.
Arguments:
- field: float32 [33, 32, 672, 256], P(None, 'gx', 'gy', 'sa'), as said below
- start: float32 [33, 16], replicated, may hold values from -1 to 1
Outputs:
- basis: float32 [33, 16], replicated
- gram_two: float32 [672, 672], P('gy', ('gx', 'sa'))
Inputs may be any that keep to these rules, and one draw needn't show every extreme that they name: `field`: every entry is finite; species differ in scale.
All inputs are finite; a program needn't handle non-finite values.
Results may differ from a plain program's by a relative error of at most 0.0003.
Values sent between devices are 32-bit elements; how exact they have to be, the bound alone decides.
A program may use at most 128 MiB of HBM per device.

v0:
```python
import jax
import jax.numpy as jnp
from jax import lax
from jax.sharding import PartitionSpec as P

ITERS = 4
HIGH = lax.Precision.HIGHEST


def orth(block):
    inner = jnp.dot(block.T, block, precision=HIGH, preferred_element_type=jnp.float32)
    lower = jnp.linalg.cholesky(inner)
    return jax.scipy.linalg.solve_triangular(lower, block.T, lower=True).T


def leading(gram, start, rounds):
    basis = orth(orth(start))
    for step in range(rounds):
        basis = orth(orth(jnp.dot(gram, basis, precision=HIGH, preferred_element_type=jnp.float32)))
    return basis


def project(basis, data):
    return jnp.einsum("sr,sxyz->rxyz", basis, data, precision=HIGH)


def line_gram(left, right):
    return jnp.einsum("rxiz,rxjz->ij", left, right, precision=HIGH)


def on_device(field, start):
    species, cells_x, cells_y, cells_z = field.shape
    ranks = start.shape[1]
    total_x = cells_x * lax.axis_size("gx")
    total_y = cells_y * lax.axis_size("gy")
    total_z = cells_z * lax.axis_size("sa")
    flat = field.reshape(species, -1)
    partial_gram = jnp.dot(flat, flat.T, precision=HIGH, preferred_element_type=jnp.float32)
    species_gram = lax.psum(partial_gram, ("gx", "gy", "sa")) / (total_x * total_y * total_z)
    basis = leading(species_gram, start, ITERS)
    core = project(basis, field)
    part_block = line_gram(core, lax.all_gather(core, "gy", axis=2, tiled=True))
    block = lax.psum_scatter(part_block, ("gx", "sa"), scatter_dimension=1, tiled=True) / (
        ranks * total_x * total_z
    )
    return (basis, block)


def solution(mesh):
    in_specs = (P(None, "gx", "gy", "sa"), P())
    out_specs = (P(), P("gy", ("gx", "sa")))
    return jax.shard_map(
        on_device, mesh=mesh, in_specs=in_specs, out_specs=out_specs, check_vma=False
    )
```

profile of v0, /device:TPU:1, one launch (start us, length us, event | category | flops | bytes accessed | tf_op | source)
XLA Modules:
  0.0 422.5 jit_solution(17980562996375337005)
XLA Ops:
  7.2 0.6 copy-done
  8.1 1.5 cholesky.164
  9.6 0.6 compare_reduce_fusion.9
  10.2 0.6 fusion.27
  10.9 1.2 custom-call.14
  12.1 0.2 fusion.69
  12.5 1.5 cholesky.175
  14.0 0.6 compare_reduce_fusion.8
  14.7 0.6 fusion.28
  15.3 1.2 custom-call.15
  16.6 0.2 fusion.66
  16.8 6.2 %fusion.12 = f32[33,33]{1,0:T(8,128)S(1)} fusion(f32[33,4,42,128]{3,1,2,0:T(4,128)} %param.5), kind=kOutput, calls=%fused_computation.8 | convolution fusion | flops 281014272 | bytes 2842884 | tf_op jit(solution)/shard_map/dot_general | solution.py:38
  22.9 81.5 %psum.7 = f32[33,33]{1,0:T(8,128)S(1)} all-reduce(f32[33,33]{1,0:T(8,128)S(1)} %fusion.12), channel_id=1, replica_groups=mesh['gx'=8,'gy'=16,'sa'=2] {'gx','gy','sa'}, use_global_device_ids=true, to_apply=%region_0.0 | all-reduce | flops 1089 | bytes 8712 | tf_op jit(solution)/shard_map/psum | solution.py:39
  104.6 0.1 fusion.97
  104.8 1.5 cholesky.186
  106.3 0.6 compare_reduce_fusion.7
  107.0 0.6 fusion.29
  107.6 1.2 custom-call.16
  108.9 0.2 fusion.62
  109.3 1.5 cholesky.197
  110.8 0.6 compare_reduce_fusion.6
  111.4 0.6 fusion.30
  112.1 1.2 custom-call.17
  113.3 0.2 fusion.59
  113.5 0.2 fusion.19
  113.9 1.5 cholesky.208
  115.4 0.6 compare_reduce_fusion.5
  116.0 0.6 fusion.31
  116.7 1.2 custom-call.18
  117.9 0.2 fusion.55
  118.4 1.5 cholesky.219
  119.9 0.6 compare_reduce_fusion.4
  120.5 0.6 fusion.32
  121.2 1.2 custom-call.19
  122.4 0.2 fusion.52
  122.6 0.2 fusion.17
  123.0 1.5 cholesky.230
  124.5 0.6 compare_reduce_fusion.3
  125.1 0.6 fusion.33
  125.8 1.2 custom-call.20
  127.0 0.2 fusion.48
  127.4 1.5 cholesky.241
  128.9 0.6 compare_reduce_fusion.2
  129.6 0.6 fusion.34
  130.2 1.2 custom-call.21
  131.5 0.2 fusion.45
  131.7 0.2 fusion.15
  132.0 1.5 cholesky.252
  133.5 0.6 compare_reduce_fusion.1
  134.2 0.6 fusion.35
  134.9 1.2 custom-call.22
  136.1 0.2 fusion.41
  136.5 1.5 cholesky.263
  138.0 0.6 compare_reduce_fusion
  138.7 0.6 fusion.36
  139.3 1.2 custom-call.23
  140.5 0.2 fusion.38
  140.8 3.4 fusion.2
  144.2 0.2 all-reduce.3.cloned.1.call-start
  144.4 138.0 %all-gather.2.cloned.1.call-done = f32[16,4,672,128]{3,0,2,1:T(8,128)} async-done(((f32[16,4,42,128]{3,0,2,1:T(8,128)}), f32[16,4,672,128]{3,0,2,1:T(8,128)}) %all-gather.2.cloned.1.call-update) | async-done | bytes 22020112 | tf_op jit(solution)/shard_map/all_gather | solution.py:42
  282.4 29.2 %fusion.7 = f32[42,672]{1,0:T(8,128)} fusion(f32[16,4,672,128]{3,0,2,1:T(8,128)} %all-gather.2.cloned.1.call-done, f32[16,4,42,128]{3,0,2,1:T(8,128)} %fusion.2), kind=kOutput, calls=%fused_computation.7 | convolution fusion | flops 2774532096 | bytes 23509248 | tf_op jit(solution)/shard_map/rxiz,rxjz->ij/dot_general | solution.py:28
  311.6 0.6 dynamic-slice
  312.9 101.3 %all-reduce.3.cloned.1.call-done = f32[42,672]{1,0:T(8,128)} async-done(((f32[42,672]{1,0:T(8,128)}), f32[42,672]{1,0:T(8,128)}) %all-reduce.3.cloned.1.call-update) | async-done | bytes 112912
  414.2 1.5 dynamic-slice_multiply_fusion
  (50 shorter events, 2.6 us)
Async XLA Ops:
  7.2 0.7 copy-start
  7.2 133.6 %copy-start.1 = (f32[33,4,42,128]{3,1,2,0:T(4,128)S(1)}, f32[33,4,42,128]{3,1,2,0:T(4,128)}, u32[]{:S(2)}) copy-start(f32[33,4,42,128]{3,1,2,0:T(4,128)} %param.5) | copy-start | bytes 8515588
  7.2 275.2 %all-gather.2.cloned.1.call-start = ((), (), s32[]{:S(2)}) async-start(), calls=%async_computation | async-start | bytes 23396352 | tf_op jit(solution)/shard_map/all_gather | solution.py:42
  140.7 3.4 copy-start.2
  144.2 167.4 %copy-start.3 = (u32[256]{0:T(256)S(1)}, u32[256]{0:T(256)}, u32[]{:S(2)}) copy-start(u32[256]{0:T(256)} %constant.40) | copy-start | bytes 3076
  144.2 270.0 %all-reduce.3.cloned.1.call-start = ((), (), s32[]{:S(2)}) async-start(), calls=%async_computation.1 | async-start | bytes 294912
Sparse Core Ops, SparseCore 0:
  144.3 138.0 all-gather.1
  311.7 102.3 all-reduce.2
where the time goes:
time: 423 us; the launch traced here: 422 us
  waiting for transfers between devices  239 us (57%)
  blocking collectives  81.5 us (19%)
  matrix products  42.7 us (10%)
  other arithmetic  41.8 us (10%)
  between operations  14.9 us (4%)
    all_gather x1, waiting for transfers between devices, on_device(): part_block = line_gram(core, lax.all_gather(core, 'gy', axis=2, tiled=True))  138 us
    unnamed x3, waiting for transfers between devices  101 us
    psum x1, blocking collectives, on_device(): lax.psum(partial_gram, ('gx', 'gy', 'sa')) / (total_x * total_y * total_z)  81.5 us
    dot_general x1, matrix products, line_gram(): return jnp.einsum('rxiz,rxjz->ij', left, right, precision=HIGH)  29.2 us
    another operation x30, other arithmetic, orth(): lower = jnp.linalg.cholesky(inner)  21.5 us
    another operation x20, other arithmetic, orth(): return jax.scipy.linalg.solve_triangular(lower, block.T, lower=True).T  18.8 us
  transfers between devices with their start and end apart: 2, of which 2 were waited for; matrix products, arithmetic and copies ran while one was open for 0% of the time, Pallas kernels for 0%

commit v1 on v0

--- a/solution.py
+++ b/solution.py
@@ -36,7 +36,9 @@
     total_z = cells_z * lax.axis_size("sa")
     flat = field.reshape(species, -1)
     partial_gram = jnp.dot(flat, flat.T, precision=HIGH, preferred_element_type=jnp.float32)
-    species_gram = lax.psum(partial_gram, ("gx", "gy", "sa")) / (total_x * total_y * total_z)
+    species_gram = jnp.sum(lax.all_gather(partial_gram, ("gx", "gy", "sa")), axis=0) / (
+        total_x * total_y * total_z
+    )
     basis = leading(species_gram, start, ITERS)
     core = project(basis, field)
     part_block = line_gram(core, lax.all_gather(core, "gy", axis=2, tiled=True))

time: 423 us -> 457 us (1.080)
  waiting for transfers between devices: 239 us -> 352 us
  blocking collectives: 81.5 us -> 0 us
    all_gather x0 -> x1, waiting for transfers between devices: none -> 112 us  [on_device(): lax.all_gather(partial_gram, ('gx', 'gy', 'sa'))]
    psum x1 -> x0, blocking collectives: 81.5 us -> none  [on_device(): lax.psum(partial_gram, ('gx', 'gy', 'sa')) / (total_x * total_y * total_z)]
    unnamed x3 -> x4, waiting for transfers between devices: 101 us -> 101 us
  transfers between devices with their start and end apart: 2 -> 3, of which waited for: 2 -> 3; matrix products, arithmetic and copies ran while one was open for 0% -> 2% of each run, Pallas kernels for 0% -> 0%
where the time goes in v1:
time: 457 us
  waiting for transfers between devices  352 us (77%)
  other arithmetic  44.8 us (10%)
  matrix products  43.3 us (9%)
  between operations  14.6 us (3%)
    all_gather x1, waiting for transfers between devices, on_device(): part_block = line_gram(core, lax.all_gather(core, 'gy', axis=2, tiled=True))  140 us
    all_gather x1, waiting for transfers between devices, on_device(): lax.all_gather(partial_gram, ('gx', 'gy', 'sa'))  112 us
    unnamed x4, waiting for transfers between devices  101 us
    dot_general x1, matrix products, line_gram(): return jnp.einsum('rxiz,rxjz->ij', left, right, precision=HIGH)  29.2 us
    another operation x30, other arithmetic, orth(): lower = jnp.linalg.cholesky(inner)  21.5 us
    another operation x20, other arithmetic, orth(): return jax.scipy.linalg.solve_triangular(lower, block.T, lower=True).T  18.8 us
  transfers between devices with their start and end apart: 3, of which 3 were waited for; matrix products, arithmetic and copies ran while one was open for 2% of the time, Pallas kernels for 0%

profile of v1, /device:TPU:1, one launch (start us, length us, event | category | flops | bytes accessed | tf_op | source)
XLA Modules:
  0.0 456.8 jit_solution(11824041834173788963)
XLA Ops:
  7.2 6.8 %fusion.12 = f32[1,33,33]{2,1,0:T(8,128)} fusion(f32[33,4,42,128]{3,1,2,0:T(4,128)} %param.5), kind=kOutput, calls=%fused_computation.8 | convolution fusion | flops 281014272 | bytes 2842884 | tf_op jit(solution)/shard_map/dot_general | solution.py:38
  14.3 1.5 cholesky.164
  15.8 0.6 compare_reduce_fusion.9
  16.4 0.6 fusion.27
  17.1 1.2 custom-call.14
  18.3 0.2 fusion.69
  18.7 1.5 cholesky.175
  20.2 0.6 compare_reduce_fusion.8
  20.9 0.6 fusion.28
  21.5 1.2 custom-call.15
  22.8 0.2 fusion.66
  23.0 111.5 %all-gather.7.cloned.1.call-done = f32[256,33,33]{2,1,0:T(8,128)} async-done(((f32[1,33,33]{2,1,0:T(8,128)}), f32[256,33,33]{2,1,0:T(8,128)}) %all-gather.7.cloned.1.call-update) | async-done | bytes 1115152 | tf_op jit(solution)/shard_map/all_gather | solution.py:39
  134.5 3.0 reduce_sum.9
  137.6 0.1 fusion.97
  137.8 1.5 cholesky.186
  139.3 0.6 compare_reduce_fusion.7
  140.0 0.6 fusion.29
  140.6 1.2 custom-call.16
  141.8 0.2 fusion.62
  142.3 1.5 cholesky.197
  143.8 0.6 compare_reduce_fusion.6
  144.4 0.6 fusion.30
  145.1 1.2 custom-call.17
  146.3 0.2 fusion.59
  146.5 0.2 fusion.19
  146.9 1.5 cholesky.208
  148.4 0.6 compare_reduce_fusion.5
  149.0 0.6 fusion.31
  149.7 1.2 custom-call.18
  150.9 0.2 fusion.55
  151.3 1.5 cholesky.219
  152.8 0.6 compare_reduce_fusion.4
  153.5 0.6 fusion.32
  154.2 1.2 custom-call.19
  155.4 0.2 fusion.52
  155.6 0.2 fusion.17
  156.0 1.5 cholesky.230
  157.5 0.6 compare_reduce_fusion.3
  158.1 0.6 fusion.33
  158.8 1.2 custom-call.20
  160.0 0.2 fusion.48
  160.4 1.5 cholesky.241
  161.9 0.6 compare_reduce_fusion.2
  162.6 0.6 fusion.34
  163.2 1.2 custom-call.21
  164.5 0.2 fusion.45
  164.7 0.2 fusion.15
  165.0 1.5 cholesky.252
  166.5 0.6 compare_reduce_fusion.1
  167.2 0.6 fusion.35
  167.8 1.2 custom-call.22
  169.1 0.2 fusion.41
  169.5 1.5 cholesky.263
  171.0 0.6 compare_reduce_fusion
  171.6 0.6 fusion.36
  172.3 1.2 custom-call.23
  173.5 0.2 fusion.38
  173.8 3.4 fusion.2
  177.2 0.2 all-reduce.3.cloned.1.call-start
  177.4 139.6 %all-gather.5.cloned.1.call-done = f32[16,4,672,128]{3,0,2,1:T(8,128)} async-done(((f32[16,4,42,128]{3,0,2,1:T(8,128)}), f32[16,4,672,128]{3,0,2,1:T(8,128)}) %all-gather.5.cloned.1.call-update) | async-done | bytes 22020112 | tf_op jit(solution)/shard_map/all_gather | solution.py:44
  317.1 29.2 %fusion.7 = f32[42,672]{1,0:T(8,128)} fusion(f32[16,4,672,128]{3,0,2,1:T(8,128)} %all-gather.5.cloned.1.call-done, f32[16,4,42,128]{3,0,2,1:T(8,128)} %fusion.2), kind=kOutput, calls=%fused_computation.7 | convolution fusion | flops 2774532096 | bytes 23509248 | tf_op jit(solution)/shard_map/rxiz,rxjz->ij/dot_general | solution.py:28
  346.3 0.6 dynamic-slice
  347.5 101.3 %all-reduce.3.cloned.1.call-done = f32[42,672]{1,0:T(8,128)} async-done(((f32[42,672]{1,0:T(8,128)}), f32[42,672]{1,0:T(8,128)}) %all-reduce.3.cloned.1.call-update) | async-done | bytes 112912
  448.8 1.5 dynamic-slice_multiply_fusion
  (53 shorter events, 2.7 us)
Async XLA Ops:
  7.2 6.9 %copy-start = (f32[33,16]{0,1:T(8,128)S(1)}, f32[33,16]{0,1:T(8,128)}, u32[]{:S(2)}) copy-start(f32[33,16]{0,1:T(8,128)} %param.6) | copy-start | bytes 6340
  7.2 127.3 %all-gather.7.cloned.1.call-start = ((), (), s32[]{:S(2)}) async-start(), calls=%async_computation.1 | async-start | bytes 5263360 | tf_op jit(solution)/shard_map/all_gather | solution.py:39
  14.0 303.1 %all-gather.5.cloned.1.call-start = ((), (), s32[]{:S(2)}) async-start(), calls=%async_computation | async-start | bytes 23396352 | tf_op jit(solution)/shard_map/all_gather | solution.py:44
  23.0 150.8 %copy-start.1 = (f32[33,4,42,128]{3,1,2,0:T(4,128)S(1)}, f32[33,4,42,128]{3,1,2,0:T(4,128)}, u32[]{:S(2)}) copy-start(f32[33,4,42,128]{3,1,2,0:T(4,128)} %param.5) | copy-start | bytes 8515588
  173.7 3.4 copy-start.2
  177.2 169.1 %copy-start.3 = (u32[256]{0:T(256)S(1)}, u32[256]{0:T(256)}, u32[]{:S(2)}) copy-start(u32[256]{0:T(256)} %constant.42) | copy-start | bytes 3076
  177.2 271.6 %all-reduce.3.cloned.1.call-start = ((), (), s32[]{:S(2)}) async-start(), calls=%async_computation.2 | async-start | bytes 294912
Sparse Core Ops, SparseCore 0:
  14.1 120.2 all-gather.6
  177.3 139.7 all-gather.4
  346.4 102.3 all-reduce.2
